TPU v7x, 32 devices: a whole 2x2x4 slice. The times are simulated.
32 devices in a mesh: dp: 2 (over core), expert: 16 (over z, y, x).
Axes of the slice: x: 2, y: 2, z: 4, core: 2. Of those that a mesh axis runs over, the one named last changes fastest.
Arguments:
- tokens: bfloat16 [4096, 2048], P(('dp', 'expert')), may hold values from -6 to 6
- grad_out: bfloat16 [4096, 2048], P(('dp', 'expert')), may hold values from -6 to 6
- expert_ids: int32 [4096, 4], P(('dp', 'expert')), may hold values from 0 to 15, all different within a row; in each aligned block of 128 rows (0 to 127, 128 to 255, ...) at most 40 rows name the same one
- gate_values: bfloat16 [4096, 4], P(('dp', 'expert')), may hold values from 0.019897461 to 0.796875
- weight_in: bfloat16 [16, 2, 1408, 2048], P('expert', None, 'dp'), may hold values from -0.125 to 0.125
- weight_down: bfloat16 [16, 1408, 2048], P('expert', 'dp'), may hold values from -0.15625 to 0.15625
Outputs:
- grad_tokens: bfloat16 [4096, 2048], P(('dp', 'expert'))
- grad_gates: bfloat16 [4096, 4], P(('dp', 'expert'))
- grad_weight_in: bfloat16 [16, 2, 1408, 2048], P('expert', None, 'dp')
- grad_weight_down: bfloat16 [16, 1408, 2048], P('expert', 'dp')
Inputs may be any that keep to these rules, and one draw needn't show every extreme that they name: `expert_ids`: each row names 4 different experts. Within each aligned block of 128 rows (the rows of one device) no expert is named by more than 40 rows, and in some block some expert is named by exactly 40 rows.
All inputs are finite; a program needn't handle non-finite values.
Results may differ from a plain program's by a relative error of at most 0.008.
Values may be sent and summed in bfloat16 or wider, within the bound.
A program may use at most 128 MiB of HBM per device.

v0:
```python
import jax
import jax.numpy as jnp
from jax import lax
from jax.sharding import PartitionSpec as P


def expert_grads(inputs_rows, dy_rows, gate_rows, proj_in, proj_down):
    hidden = proj_in.shape[1]
    stacked = proj_in.reshape(2 * hidden, proj_in.shape[2])
    projected = lax.dot_general(
        inputs_rows, stacked, (((1,), (1,)), ((), ())), preferred_element_type=jnp.float32
    )
    gate_part = projected[:, :hidden]
    up_part = projected[:, hidden:]
    sigmoid_gate = jax.nn.sigmoid(gate_part)
    silu_gate = gate_part * sigmoid_gate
    hidden_act = (silu_gate * up_part).astype(jnp.bfloat16)
    upstream = lax.dot_general(
        dy_rows, proj_down, (((1,), (1,)), ((), ())), preferred_element_type=jnp.float32
    )
    gate_grad = jnp.sum(upstream * hidden_act.astype(jnp.float32), axis=1)
    gate_scale = gate_rows.astype(jnp.float32)[:, None]
    scaled_dy = (gate_scale * dy_rows.astype(jnp.float32)).astype(jnp.bfloat16)
    grad_down = lax.dot_general(
        hidden_act, scaled_dy, (((0,), (0,)), ((), ())), preferred_element_type=jnp.float32
    )
    hidden_grad = gate_scale * upstream
    grad_gate_part = (
        hidden_grad * up_part * sigmoid_gate * (1.0 + gate_part * (1.0 - sigmoid_gate))
    ).astype(jnp.bfloat16)
    grad_up_part = (hidden_grad * silu_gate).astype(jnp.bfloat16)
    joined = jnp.concatenate([grad_gate_part, grad_up_part], axis=1)
    row_grads = jnp.dot(joined, stacked, preferred_element_type=jnp.float32)
    grad_in = lax.dot_general(
        joined, inputs_rows, (((0,), (0,)), ((), ())), preferred_element_type=jnp.float32
    )
    return (row_grads, gate_grad, grad_in.reshape(2, hidden, proj_in.shape[2]), grad_down)


def slot_places(expert_ids, experts, capacity):
    flat_ids = expert_ids.reshape(-1)
    onehot = (flat_ids[:, None] == jnp.arange(experts, dtype=jnp.int32)[None, :]).astype(jnp.int32)
    running = jnp.cumsum(onehot, axis=0) - 1
    position = jnp.sum(onehot * running, axis=1)
    return flat_ids * capacity + position


def body(tokens, grad_out, expert_ids, gate_values, weight_in, weight_down):
    experts = lax.axis_size("expert")
    tok_rows = tokens.shape[0]
    feature_count = tokens.shape[1]
    top_count = expert_ids.shape[1]
    capacity = tok_rows * top_count * 5 // (4 * experts)
    slot_count = experts * capacity
    slot_index = slot_places(expert_ids, experts, capacity)
    pair_count = tok_rows * top_count
    owner_pair = (
        jnp.full((slot_count,), pair_count, jnp.int32)
        .at[slot_index]
        .set(jnp.arange(pair_count, dtype=jnp.int32))
    )
    token_of = owner_pair // top_count
    pad_row = jnp.zeros((1, feature_count), jnp.bfloat16)
    send_inputs = jnp.concatenate([tokens, pad_row], axis=0)[token_of].reshape(
        experts, capacity, feature_count
    )
    send_dy = jnp.concatenate([grad_out, pad_row], axis=0)[token_of].reshape(
        experts, capacity, feature_count
    )
    send_gate = jnp.concatenate([gate_values.reshape(-1), jnp.zeros((1,), jnp.bfloat16)])[
        owner_pair
    ].reshape(experts, capacity)
    recv_inputs, recv_dy, recv_gate = (
        lax.all_to_all(send_inputs, "expert", split_axis=0, concat_axis=0, tiled=True),
        lax.all_to_all(send_dy, "expert", split_axis=0, concat_axis=0, tiled=True),
        lax.all_to_all(send_gate, "expert", split_axis=0, concat_axis=0, tiled=True),
    )
    full_in, full_down = (
        lax.all_gather(weight_in, "dp", axis=2, tiled=True),
        lax.all_gather(weight_down, "dp", axis=1, tiled=True),
    )
    row_grads, gate_grad, grad_in, grad_down = expert_grads(
        recv_inputs.reshape(slot_count, feature_count),
        recv_dy.reshape(slot_count, feature_count),
        recv_gate.reshape(slot_count),
        full_in[0],
        full_down[0],
    )
    grad_in, grad_down = (
        lax.psum_scatter(grad_in, "dp", scatter_dimension=1, tiled=True),
        lax.psum_scatter(grad_down, "dp", scatter_dimension=0, tiled=True),
    )
    back_rows, back_gate = (
        lax.all_to_all(
            row_grads.astype(jnp.bfloat16).reshape(experts, capacity, feature_count),
            "expert",
            split_axis=0,
            concat_axis=0,
            tiled=True,
        ),
        lax.all_to_all(
            gate_grad.astype(jnp.bfloat16).reshape(experts, capacity),
            "expert",
            split_axis=0,
            concat_axis=0,
            tiled=True,
        ),
    )
    picked = back_rows.reshape(slot_count, feature_count)[slot_index].reshape(
        tok_rows, top_count, feature_count
    )
    grad_tokens = jnp.sum(picked, axis=1, dtype=jnp.float32).astype(jnp.bfloat16)
    grad_gates = back_gate.reshape(slot_count)[slot_index].reshape(tok_rows, top_count)
    return (
        grad_tokens,
        grad_gates,
        grad_in.astype(jnp.bfloat16)[None],
        grad_down.astype(jnp.bfloat16)[None],
    )


def solution(mesh):
    placed = (
        P(("dp", "expert"), None),
        P(("dp", "expert"), None),
        P(("dp", "expert"), None),
        P(("dp", "expert"), None),
        P("expert", None, "dp", None),
        P("expert", "dp", None),
    )
    return jax.shard_map(
        body,
        mesh=mesh,
        in_specs=placed,
        out_specs=(
            P(("dp", "expert"), None),
            P(("dp", "expert"), None),
            P("expert", None, "dp", None),
            P("expert", "dp", None),
        ),
        check_vma=False,
    )
```

profile of v0, /device:TPU:12, one launch (start us, length us, event | category | flops | bytes accessed | tf_op | source)
XLA Modules:
  0.0 318.7 jit_solution(16413516991251456437)
XLA Ops:
  7.2 0.7 all-gather.5.cloned.1.call-update
  8.8 1.2 reduce-window.6
  10.3 2.4 scatter_custom_fusion
  12.8 4.3 %gather_fusion = bf16[640]{0:T(1024)(128)(2,1)S(1)} fusion(bf16[513]{0:T(1024)(128)(2,1)S(1)} %pad_maximum_fusion.2, s32[1024]{0:T(1024)S(1)} %get-tuple-element.21), kind=kCustom, calls=%fused_computation | custom fusion | bytes 5120 | tf_op jit(solution)/shard_map/gather | solution.py:70
  17.1 0.7 all_to_all.25
  17.8 7.2 %all-to-all-start = ((bf16[16,1,40]{2,1,0:T(2,128)(2,1)}), bf16[16,1,40]{2,1,0:T(2,128)(2,1)S(1)}, u32[]{:S(2)}, u32[]{:S(2)}) async-start(bf16[16,1,40]{2,1,0:T(2,128)(2,1)} %all_to_all.25), calls=%async_computation | async-start | bytes 16384 | tf_op jit(solution)/shard_map/all_to_all | solution.py:76
  25.1 4.1 %gather_fusion.2 = bf16[640,2048]{1,0:T(8,128)(2,1)} fusion(bf16[129,2048]{1,0:T(8,128)(2,1)S(1)} %concatenate.14, s32[1024]{0:T(1024)S(1)} %get-tuple-element.20), kind=kCustom, calls=%fused_computation.2 | custom fusion | bytes 5245440 | tf_op jit(solution)/shard_map/gather | solution.py:64
  29.1 0.8 all-to-all-done
  29.9 6.1 %all-to-all-start.2 = ((bf16[16,40,2048]{2,1,0:T(8,128)(2,1)}), bf16[16,40,2048]{2,1,0:T(8,128)(2,1)S(1)}, u32[]{:S(2)}, u32[]{:S(2)}) async-start(bf16[16,40,2048]{2,1,0:T(8,128)(2,1)} %bitcast.6), calls=%async_computation.2 | async-start | bytes 5242880 | tf_op jit(solution)/shard_map/all_to_all | solution.py:74
  36.1 0.7 all-gather.3.cloned.1.call-update
  36.8 1.1 concatenate.13
  37.9 4.1 %gather_fusion.1 = bf16[640,2048]{1,0:T(8,128)(2,1)} fusion(bf16[129,2048]{1,0:T(8,128)(2,1)S(1)} %concatenate.13, s32[1024]{0:T(1024)S(1)} %get-tuple-element.20), kind=kCustom, calls=%fused_computation.1 | custom fusion | bytes 5245440 | tf_op jit(solution)/shard_map/gather | solution.py:67
  41.9 53.0 %all-to-all-done.2 = bf16[16,40,2048]{2,1,0:T(8,128)(2,1)S(1)} async-done(((bf16[16,40,2048]{2,1,0:T(8,128)(2,1)}), bf16[16,40,2048]{2,1,0:T(8,128)(2,1)S(1)}, u32[]{:S(2)}, u32[]{:S(2)}) %all-to-all-start.2) | async-done | bytes 2621472 | tf_op jit(solution)/shard_map/all_to_all | solution.py:74
  94.9 4.8 %all-to-all-start.1 = ((bf16[16,40,2048]{2,1,0:T(8,128)(2,1)}), bf16[16,40,2048]{2,1,0:T(8,128)(2,1)}, u32[]{:S(2)}, u32[]{:S(2)}) async-start(bf16[16,40,2048]{2,1,0:T(8,128)(2,1)} %bitcast.3), calls=%async_computation.1 | async-start | bytes 5242880 | tf_op jit(solution)/shard_map/all_to_all | solution.py:75
  100.1 13.1 %fusion.14 = f32[640,2816]{1,0:T(8,128)} fusion(bf16[640,2048]{1,0:T(8,128)(2,1)S(1)} %bitcast.48, bf16[2816,2048]{1,0:T(8,128)(2,1)} %bitcast.54), kind=kOutput, calls=%fused_computation.49 | convolution fusion | flops 7381975040 | bytes 21364736 | tf_op jit(solution)/shard_map/dot_general | solution.py:10
  113.1 45.3 %all-to-all-done.1 = bf16[16,40,2048]{2,1,0:T(8,128)(2,1)} async-done(((bf16[16,40,2048]{2,1,0:T(8,128)(2,1)}), bf16[16,40,2048]{2,1,0:T(8,128)(2,1)}, u32[]{:S(2)}, u32[]{:S(2)}) %all-to-all-start.1) | async-done | bytes 2621472 | tf_op jit(solution)/shard_map/all_to_all | solution.py:75
  158.4 12.4 %multiply_reduce_fusion = (bf16[640]{0:T(1024)(128)(2,1)S(1)}, bf16[640,1408]{1,0:T(8,128)(2,1)S(1)}, bf16[640,1408]{1,0:T(8,128)(2,1)}, bf16[640,1408]{1,0:T(8,128)(2,1)}) fusion(f32[640,2816]{1,0:T(8,128)} %fusion.14, f32[640]{0:T(1024)S(1)} %reshape.128, bf16[640,2048]{1,0:T(8,128)(2,1)} %bitcast.4, bf16[1,1408,2048]{2,1,0:T(8,128)(2,1)} %all-gather.3.cloned.1.call-done), kind=kOutput, calls=%fused_computation.11 | convolution fusion | flops 3708108288 | bytes 21008128 | tf_op jit(solution)/shard_map/dot_general | solution.py:18
  170.8 9.5 %fusion.3 = f32[1408,2048]{1,0:T(8,128)} fusion(bf16[640,1408]{1,0:T(8,128)(2,1)S(1)} %get-tuple-element.13, bf16[640,2048]{1,0:T(8,128)(2,1)} %bitcast.4, f32[640]{0:T(1024)S(1)} %reshape.128), kind=kOutput, calls=%fused_computation.19 | convolution fusion | flops 3694919680 | bytes 15960576 | tf_op jit(solution)/shard_map/dot_general | solution.py:24
  180.7 4.1 %fusion.5 = bf16[2816,640]{0,1:T(8,128)(2,1)} fusion(bf16[640,1408]{1,0:T(8,128)(2,1)} %get-tuple-element.16, bf16[640,1408]{1,0:T(8,128)(2,1)} %get-tuple-element.17), kind=kLoop, calls=%fused_computation.21 | loop fusion | flops 7208960 | bytes 7208960 | tf_op jit(solution)/shard_map/dot_general | solution.py:34
  184.8 6.3 %copy.27 = bf16[2816,640]{1,0:T(8,128)(2,1)} copy(bf16[2816,640]{0,1:T(8,128)(2,1)} %fusion.5) | data formatting | bytes 7208960 | tf_op jit(solution)/shard_map/dot_general | solution.py:34
  191.0 15.1 %fusion.15 = f32[2,1408,2048]{2,1,0:T(8,128)} fusion(bf16[2,1408,640]{2,1,0:T(8,128)(2,1)} %bitcast.47, bf16[640,2048,1]{1,0,2:T(8,128)(2,1)S(1)} %bitcast.49), kind=kOutput, calls=%fused_computation.50 | convolution fusion | flops 7381975040 | bytes 29294592 | tf_op jit(solution)/shard_map/dot_general | solution.py:34
  206.2 0.7 convert_element_type.73
  206.9 5.3 %all-to-all-start.4 = ((bf16[16,1,40]{2,1,0:T(2,128)(2,1)}), bf16[16,1,40]{2,1,0:T(2,128)(2,1)S(1)}, u32[]{:S(2)}, u32[]{:S(2)}) async-start(bf16[16,1,40]{2,1,0:T(2,128)(2,1)} %convert_element_type.73), calls=%async_computation.4 | async-start | bytes 16384 | tf_op jit(solution)/shard_map/all_to_all | solution.py:101
  212.2 13.0 %convolution_convert_fusion = bf16[640,2048]{1,0:T(8,128)(2,1)} fusion(bf16[2816,2048]{1,0:T(8,128)(2,1)} %bitcast.55, bf16[640,1408]{1,0:T(8,128)(2,1)S(1)} %copy-done, bf16[640,1408]{1,0:T(8,128)(2,1)} %get-tuple-element.17), kind=kOutput, calls=%fused_computation.17 | convolution fusion | flops 7390494720 | bytes 17760256 | tf_op jit(solution)/shard_map/dot_general | solution.py:33
  225.2 6.9 %all-to-all-start.3 = ((bf16[16,40,2048]{2,1,0:T(8,128)(2,1)}), bf16[16,40,2048]{2,1,0:T(8,128)(2,1)S(1)}, u32[]{:S(2)}, u32[]{:S(2)}) async-start(bf16[16,40,2048]{2,1,0:T(8,128)(2,1)} %bitcast.50), calls=%async_computation.3 | async-start | bytes 5242880 | tf_op jit(solution)/shard_map/all_to_all | solution.py:94
  232.2 3.5 %gather_fusion.4 = bf16[512]{0:T(512)(128)(2,1)S(1)} fusion(bf16[640]{0:T(1024)(128)(2,1)S(1)} %reshape.126, s32[1024]{0:T(1024)S(1)} %pad_clamp_fusion), kind=kCustom, calls=%fused_computation.4 | custom fusion | bytes 4096 | tf_op jit(solution)/shard_map/gather | solution.py:113
  236.5 53.4 %all-to-all-done.3 = bf16[16,40,2048]{2,1,0:T(8,128)(2,1)S(1)} async-done(((bf16[16,40,2048]{2,1,0:T(8,128)(2,1)}), bf16[16,40,2048]{2,1,0:T(8,128)(2,1)S(1)}, u32[]{:S(2)}, u32[]{:S(2)}) %all-to-all-start.3) | async-done | bytes 2621472 | tf_op jit(solution)/shard_map/all_to_all | solution.py:94
  290.0 3.3 %gather_fusion.3 = bf16[512,2048]{1,0:T(8,128)(2,1)} fusion(bf16[640,2048]{1,0:T(8,128)(2,1)S(1)} %bitcast.46, s32[1024]{0:T(1024)S(1)} %pad_clamp_fusion), kind=kCustom, calls=%fused_computation.3 | custom fusion | bytes 4196352 | tf_op jit(solution)/shard_map/gather | solution.py:109
  293.2 2.7 reshape.125
  296.0 3.9 %reduce_sum.34 = bf16[128,2048]{1,0:T(8,128)(2,1)} reduce(bf16[128,4,2048]{2,1,0:T(4,128)(2,1)S(1)} %reshape.125, bf16[]{:T(256)} %constant.37.clone.1), dimensions={1}, to_apply=%region_4.5 | reduce | flops 786432 | bytes 2621442 | tf_op jit(solution)/shard_map/reduce_sum | solution.py:112
  299.8 4.7 %convert_bitcast_fusion.1 = bf16[1,704,2048]{2,1,0:T(8,128)(2,1)} fusion(f32[704,2048]{1,0:T(8,128)} %reduce-scatter.5.cloned.1.call-done), kind=kLoop, calls=%fused_computation.18 | loop fusion | flops 1441792 | bytes 8650752 | tf_op jit(solution)/shard_map/broadcast_in_dim | solution.py:118
  304.5 7.7 %convert_bitcast_fusion = bf16[1,2,704,2048]{3,2,1,0:T(8,128)(2,1)} fusion(f32[2,704,2048]{2,1,0:T(8,128)} %reduce-scatter.3.cloned.1.call-done), kind=kLoop, calls=%fused_computation.8 | loop fusion | flops 2883584 | bytes 17301504 | tf_op jit(solution)/shard_map/broadcast_in_dim | solution.py:117
  (45 shorter events, 2.9 us)
Async XLA Ops:
  7.2 0.8 copy-start.2
  7.2 1.1 copy-start.3
  7.2 17.8 %copy-start.1 = (bf16[128,2048]{1,0:T(8,128)(2,1)S(1)}, bf16[128,2048]{1,0:T(8,128)(2,1)}, u32[]{:S(2)}) copy-start(bf16[128,2048]{1,0:T(8,128)(2,1)} %param.6) | copy-start | bytes 1572868
  7.2 92.9 %all-gather.5.cloned.1.call-start = ((), (), s32[]{:S(2)}) async-start(), calls=%async_computation.8 | async-start | bytes 17301504 | tf_op jit(solution)/shard_map/all_gather | solution.py:79
  17.8 12.1 %all-to-all-start = ((bf16[16,1,40]{2,1,0:T(2,128)(2,1)}), bf16[16,1,40]{2,1,0:T(2,128)(2,1)S(1)}, u32[]{:S(2)}, u32[]{:S(2)}) async-start(bf16[16,1,40]{2,1,0:T(2,128)(2,1)} %all_to_all.25), calls=%async_computation | async-start | bytes 16384 | tf_op jit(solution)/shard_map/all_to_all | solution.py:76
  29.9 65.0 %all-to-all-start.2 = ((bf16[16,40,2048]{2,1,0:T(8,128)(2,1)}), bf16[16,40,2048]{2,1,0:T(8,128)(2,1)S(1)}, u32[]{:S(2)}, u32[]{:S(2)}) async-start(bf16[16,40,2048]{2,1,0:T(8,128)(2,1)} %bitcast.6), calls=%async_computation.2 | async-start | bytes 5242880 | tf_op jit(solution)/shard_map/all_to_all | solution.py:74
  36.0 122.4 %all-gather.3.cloned.1.call-start = ((), (), s32[]{:S(2)}) async-start(), calls=%async_computation.7 | async-start | bytes 8650752 | tf_op jit(solution)/shard_map/all_gather | solution.py:80
  94.9 63.5 %all-to-all-start.1 = ((bf16[16,40,2048]{2,1,0:T(8,128)(2,1)}), bf16[16,40,2048]{2,1,0:T(8,128)(2,1)}, u32[]{:S(2)}, u32[]{:S(2)}) async-start(bf16[16,40,2048]{2,1,0:T(8,128)(2,1)} %bitcast.3), calls=%async_computation.1 | async-start | bytes 5242880 | tf_op jit(solution)/shard_map/all_to_all | solution.py:75
  99.7 200.1 %reduce-scatter.5.cloned.1.call-start = ((), (), s32[]{:S(2)}) async-start(), calls=%async_computation.10 | async-start | bytes 17301504 | tf_op jit(solution)/shard_map/reduce_scatter | solution.py:91
  180.4 124.1 %reduce-scatter.3.cloned.1.call-start = ((), (), s32[]{:S(2)}) async-start(), calls=%async_computation.9 | async-start | bytes 34603008 | tf_op jit(solution)/shard_map/reduce_scatter | solution.py:90
  206.2 6.0 %copy-start = (bf16[640,1408]{1,0:T(8,128)(2,1)S(1)}, bf16[640,1408]{1,0:T(8,128)(2,1)}, u32[]{:S(2)}) copy-start(bf16[640,1408]{1,0:T(8,128)(2,1)} %get-tuple-element.16) | copy-start | bytes 5406724
  206.9 18.3 %all-to-all-start.4 = ((bf16[16,1,40]{2,1,0:T(2,128)(2,1)}), bf16[16,1,40]{2,1,0:T(2,128)(2,1)S(1)}, u32[]{:S(2)}, u32[]{:S(2)}) async-start(bf16[16,1,40]{2,1,0:T(2,128)(2,1)} %convert_element_type.73), calls=%async_computation.4 | async-start | bytes 16384 | tf_op jit(solution)/shard_map/all_to_all | solution.py:101
  225.2 64.8 %all-to-all-start.3 = ((bf16[16,40,2048]{2,1,0:T(8,128)(2,1)}), bf16[16,40,2048]{2,1,0:T(8,128)(2,1)S(1)}, u32[]{:S(2)}, u32[]{:S(2)}) async-start(bf16[16,40,2048]{2,1,0:T(8,128)(2,1)} %bitcast.50), calls=%async_computation.3 | async-start | bytes 5242880 | tf_op jit(solution)/shard_map/all_to_all | solution.py:94
Sparse Core Ops, SparseCore 0:
  9.6 24.4 all-gather.4
  38.4 17.1 all-gather.2
  180.5 19.2 reduce-scatter.4
  206.3 32.5 reduce-scatter.2
where the time goes:
time: 319 us
  waiting for transfers between devices  154 us (48%)
  matrix products  63.1 us (20%)
  local copies, waits for them, and re-layouts  35.2 us (11%)
  starting transfers between devices  30.8 us (10%)
  other arithmetic  21.7 us (7%)
  between operations  14 us (4%)
    all_to_all x1, waiting for transfers between devices, body(): lax.all_to_all(row_grads.astype(jnp.bfloat16).reshape(experts, capacity,...  53.4 us
    all_to_all x1, waiting for transfers between devices, body(): lax.all_to_all(send_inputs, 'expert', split_axis=0, concat_axis=0, tiled=...  53 us
    all_to_all x1, waiting for transfers between devices, body(): lax.all_to_all(send_dy, 'expert', split_axis=0, concat_axis=0, tiled=True)  45.3 us
    dot_general x1, matrix products, expert_grads(): lax.dot_general(joined, inputs_rows, (((0,), (0,)), ((), ())), preferred_...  15.1 us
    dot_general x1, matrix products, expert_grads(): lax.dot_general(inputs_rows, stacked, (((1,), (1,)), ((), ())), preferred...  13.1 us
    dot_general x1, matrix products, expert_grads(): row_grads = jnp.dot(joined, stacked, preferred_element_type=jnp.float32)  13 us
    dot_general x1, matrix products, expert_grads(): lax.dot_general(dy_rows, proj_down, (((1,), (1,)), ((), ())), preferred_e...  12.4 us
    dot_general x1, matrix products, expert_grads(): lax.dot_general(hidden_act, scaled_dy, (((0,), (0,)), ((), ())), preferre...  9.54 us
  transfers between devices with their start and end apart: 9, of which 4 were waited for; matrix products, arithmetic and copies ran while one was open for 28% of the time, Pallas kernels for 0%

commit v1 on v0

--- a/solution.py
+++ b/solution.py
@@ -2,6 +2,38 @@
 import jax.numpy as jnp
 from jax import lax
 from jax.sharding import PartitionSpec as P
+
+
+def view_resolve(vals, where_dim, array_in):
+    found_now, local_now = (vals.shape[:where_dim], vals.shape[where_dim + 1 :])
+    return jnp.moveaxis(vals.reshape(*found_now, array_in, -1, *local_now), where_dim, 0)
+
+
+def columns_trace(packet, on_dim):
+    packet = jnp.moveaxis(packet, 0, on_dim)
+    state_now = packet.shape
+    return packet.reshape(
+        *state_now[:on_dim], state_now[on_dim] * state_now[on_dim + 1], *state_now[on_dim + 2 :]
+    )
+
+
+def face_form(t0, lane_axis, u, vector):
+    x_now = lax.axis_size(lane_axis)
+    all_values, side_arr = (x_now, lax.axis_index(lane_axis))
+    mat_out = view_resolve(t0, u, all_values)
+    seen = [mat_out[side_arr]]
+    for ii in [*range(1, all_values)]:
+        piece_now = mat_out[(side_arr + ii) % all_values]
+        seen.append(
+            lax.ppermute(
+                piece_now,
+                lane_axis,
+                [(dev_j, (dev_j + ii) % all_values) for dev_j in range(all_values)],
+            )
+        )
+    passed = jnp.stack(seen, axis=0)
+    mat_out = passed[(side_arr - jnp.arange(all_values)) % all_values]
+    return columns_trace(mat_out, vector)
 
 
 def expert_grads(inputs_rows, dy_rows, gate_rows, proj_in, proj_down):
@@ -71,7 +103,7 @@
         owner_pair
     ].reshape(experts, capacity)
     recv_inputs, recv_dy, recv_gate = (
-        lax.all_to_all(send_inputs, "expert", split_axis=0, concat_axis=0, tiled=True),
+        face_form(send_inputs, "expert", 0, 0),
         lax.all_to_all(send_dy, "expert", split_axis=0, concat_axis=0, tiled=True),
         lax.all_to_all(send_gate, "expert", split_axis=0, concat_axis=0, tiled=True),
     )

time: 319 us -> 360 us (1.13)
  starting transfers between devices: 30.8 us -> 66.8 us
  local copies, waits for them, and re-layouts: 35.2 us -> 41.6 us
  waiting for transfers between devices: 154 us -> 150 us
    ppermute x0 -> x15, waiting for transfers between devices: none -> 106 us  [face_form(): lax.ppermute(piece_now, lane_axis, [(dev_j, (dev_j + ii) % all_values) fo...]
    all_to_all x1 -> x0, waiting for transfers between devices: 53 us -> none  [body(): lax.all_to_all(send_inputs, 'expert', split_axis=0, concat_axis=0, tiled=...]
    all_to_all x1, waiting for transfers between devices: 45.3 us -> 0.01 us  [body(): lax.all_to_all(send_dy, 'expert', split_axis=0, concat_axis=0, tiled=True)]
    ppermute x0 -> x15, starting transfers between devices: none -> 34 us  [face_form(): lax.ppermute(piece_now, lane_axis, [(dev_j, (dev_j + ii) % all_values) fo...]
    all_to_all x1, waiting for transfers between devices: 53.4 us -> 43.6 us  [body(): lax.all_to_all(row_grads.astype(jnp.bfloat16).reshape(experts, capacity,...]
    all_to_all x1, starting transfers between devices: 5.29 us -> 12.1 us  [body(): lax.all_to_all(gate_grad.astype(jnp.bfloat16).reshape(experts, capacity),...]
    all_to_all x1 -> x0, starting transfers between devices: 6.09 us -> none  [body(): lax.all_to_all(send_inputs, 'expert', split_axis=0, concat_axis=0, tiled=...]
    unnamed x11 -> x35, local copies, waits for them, and re-layouts: 0.92 us -> 4.85 us
  transfers between devices with their start and end apart: 9 -> 23, of which waited for: 4 -> 11; matrix products, arithmetic and copies ran while one was open for 28% -> 27% of each run, Pallas kernels for 0% -> 0%
where the time goes in v1:
time: 360 us
  waiting for transfers between devices  150 us (42%)
  starting transfers between devices  66.8 us (19%)
  matrix products  65.5 us (18%)
  local copies, waits for them, and re-layouts  41.6 us (12%)
  other arithmetic  21.2 us (6%)
  between operations  14.4 us (4%)
    ppermute x15, waiting for transfers between devices, face_form(): lax.ppermute(piece_now, lane_axis, [(dev_j, (dev_j + ii) % all_values) fo...  106 us
    all_to_all x1, waiting for transfers between devices, body(): lax.all_to_all(row_grads.astype(jnp.bfloat16).reshape(experts, capacity,...  43.6 us
    ppermute x15, starting transfers between devices, face_form(): lax.ppermute(piece_now, lane_axis, [(dev_j, (dev_j + ii) % all_values) fo...  34 us
    dot_general x1, matrix products, expert_grads(): lax.dot_general(joined, inputs_rows, (((0,), (0,)), ((), ())), preferred_...  16.6 us
    dot_general x1, matrix products, expert_grads(): lax.dot_general(inputs_rows, stacked, (((1,), (1,)), ((), ())), preferred...  13.8 us
    dot_general x1, matrix products, expert_grads(): row_grads = jnp.dot(joined, stacked, preferred_element_type=jnp.float32)  13 us
    all_to_all x1, starting transfers between devices, body(): lax.all_to_all(gate_grad.astype(jnp.bfloat16).reshape(experts, capacity),...  12.1 us
    dot_general x1, matrix products, expert_grads(): lax.dot_general(dy_rows, proj_down, (((1,), (1,)), ((), ())), preferred_e...  11.8 us
  transfers between devices with their start and end apart: 23, of which 11 were waited for; matrix products, arithmetic and copies ran while one was open for 27% of the time, Pallas kernels for 0%

profile of v1, /device:TPU:12, one launch (start us, length us, event | category | flops | bytes accessed | tf_op | source)
XLA Modules:
  0.0 359.7 jit_solution(15887712246620612888)
XLA Ops:
  12.8 4.3 %gather_fusion = bf16[640]{0:T(1024)(128)(2,1)S(1)} fusion(bf16[513]{0:T(1024)(128)(2,1)S(1)} %pad_maximum_fusion.2, s32[1024]{0:T(1024)S(1)} %get-tuple-element.37), kind=kCustom, calls=%fused_computation | custom fusion | bytes 5120 | tf_op jit(solution)/shard_map/gather | solution.py:102
  17.8 7.2 %all-to-all-start = ((bf16[16,1,40]{2,1,0:T(2,128)(2,1)}), bf16[16,1,40]{2,1,0:T(2,128)(2,1)S(1)}, u32[]{:S(2)}, u32[]{:S(2)}) async-start(bf16[16,1,40]{2,1,0:T(2,128)(2,1)} %all_to_all.21), calls=%async_computation | async-start | bytes 16384 | tf_op jit(solution)/shard_map/all_to_all | solution.py:108
  25.3 3.4 gather_fusion.2
  38.4 4.1 %gather_fusion.1 = bf16[640,2048]{1,0:T(8,128)(2,1)} fusion(bf16[129,2048]{1,0:T(8,128)(2,1)S(1)} %concatenate.13, s32[1024]{0:T(1024)S(1)} %get-tuple-element.36), kind=kCustom, calls=%fused_computation.1 | custom fusion | bytes 5245440 | tf_op jit(solution)/shard_map/gather | solution.py:99
  42.5 6.3 %all-to-all-start.1 = ((bf16[16,40,2048]{2,1,0:T(8,128)(2,1)}), bf16[16,40,2048]{2,1,0:T(8,128)(2,1)}, u32[]{:S(2)}, u32[]{:S(2)}) async-start(bf16[16,40,2048]{2,1,0:T(8,128)(2,1)} %bitcast.3), calls=%async_computation.1 | async-start | bytes 5242880 | tf_op jit(solution)/shard_map/all_to_all | solution.py:107
  51.5 55.3 %collective-permute-done.1 = bf16[1,40,2048]{2,1,0:T(8,128)(2,1)S(1)} collective-permute-done((bf16[1,40,2048]{2,1,0:T(8,128)(2,1)}, bf16[1,40,2048]{2,1,0:T(8,128)(2,1)S(1)}, u32[]{:S(2)}, u32[]{:S(2)}) %collective-permute-start.1) | collective-permute-done | bytes 163872 | tf_op jit(solution)/shard_map/ppermute | solution.py:28
  106.8 5.3 %collective-permute-start.2 = (bf16[1,40,2048]{2,1,0:T(8,128)(2,1)}, bf16[1,40,2048]{2,1,0:T(8,128)(2,1)S(1)}, u32[]{:S(2)}, u32[]{:S(2)}) collective-permute-start(bf16[1,40,2048]{2,1,0:T(8,128)(2,1)} %get-tuple-element.30), channel_id=1, source_target_pairs={{0,3},{1,4},{2,5},{3,6},{4,7},{5,8},{6,9},{7,10},{8,11},{9,12},{10... | collective-permute-start | bytes 491528 | tf_op jit(solution)/shard_map/ppermute | solution.py:28
  112.1 3.8 %collective-permute-done.2 = bf16[1,40,2048]{2,1,0:T(8,128)(2,1)S(1)} collective-permute-done((bf16[1,40,2048]{2,1,0:T(8,128)(2,1)}, bf16[1,40,2048]{2,1,0:T(8,128)(2,1)S(1)}, u32[]{:S(2)}, u32[]{:S(2)}) %collective-permute-start.2) | collective-permute-done | bytes 163872 | tf_op jit(solution)/shard_map/ppermute | solution.py:28
  116.0 6.4 %collective-permute-done.3 = bf16[1,40,2048]{2,1,0:T(8,128)(2,1)S(1)} collective-permute-done((bf16[1,40,2048]{2,1,0:T(8,128)(2,1)}, bf16[1,40,2048]{2,1,0:T(8,128)(2,1)S(1)}, u32[]{:S(2)}, u32[]{:S(2)}) %collective-permute-start.3) | collective-permute-done | bytes 163872 | tf_op jit(solution)/shard_map/ppermute | solution.py:28
  122.4 8.3 %collective-permute-done.4 = bf16[1,40,2048]{2,1,0:T(8,128)(2,1)S(1)} collective-permute-done((bf16[1,40,2048]{2,1,0:T(8,128)(2,1)}, bf16[1,40,2048]{2,1,0:T(8,128)(2,1)S(1)}, u32[]{:S(2)}, u32[]{:S(2)}) %collective-permute-start.4) | collective-permute-done | bytes 163872 | tf_op jit(solution)/shard_map/ppermute | solution.py:28
  130.7 5.7 %collective-permute-start.5 = (bf16[1,40,2048]{2,1,0:T(8,128)(2,1)}, bf16[1,40,2048]{2,1,0:T(8,128)(2,1)S(1)}, u32[]{:S(2)}, u32[]{:S(2)}) collective-permute-start(bf16[1,40,2048]{2,1,0:T(8,128)(2,1)} %get-tuple-element.27), channel_id=1, source_target_pairs={{0,6},{1,7},{2,8},{3,9},{4,10},{5,11},{6,12},{7,13},{8,14},{9,15},... | collective-permute-start | bytes 491528 | tf_op jit(solution)/shard_map/ppermute | solution.py:28
  136.4 3.8 %collective-permute-done.5 = bf16[1,40,2048]{2,1,0:T(8,128)(2,1)S(1)} collective-permute-done((bf16[1,40,2048]{2,1,0:T(8,128)(2,1)}, bf16[1,40,2048]{2,1,0:T(8,128)(2,1)S(1)}, u32[]{:S(2)}, u32[]{:S(2)}) %collective-permute-start.5) | collective-permute-done | bytes 163872 | tf_op jit(solution)/shard_map/ppermute | solution.py:28
  140.3 4.4 %collective-permute-start.6 = (bf16[1,40,2048]{2,1,0:T(8,128)(2,1)}, bf16[1,40,2048]{2,1,0:T(8,128)(2,1)S(1)}, u32[]{:S(2)}, u32[]{:S(2)}) collective-permute-start(bf16[1,40,2048]{2,1,0:T(8,128)(2,1)} %get-tuple-element.26), channel_id=1, source_target_pairs={{0,7},{1,8},{2,9},{3,10},{4,11},{5,12},{6,13},{7,14},{8,15},{9,0},... | collective-permute-start | bytes 491528 | tf_op jit(solution)/shard_map/ppermute | solution.py:28
  144.7 4.4 %collective-permute-done.6 = bf16[1,40,2048]{2,1,0:T(8,128)(2,1)S(1)} collective-permute-done((bf16[1,40,2048]{2,1,0:T(8,128)(2,1)}, bf16[1,40,2048]{2,1,0:T(8,128)(2,1)S(1)}, u32[]{:S(2)}, u32[]{:S(2)}) %collective-permute-start.6) | collective-permute-done | bytes 163872 | tf_op jit(solution)/shard_map/ppermute | solution.py:28
  151.3 6.7 %collective-permute-done.7 = bf16[1,40,2048]{2,1,0:T(8,128)(2,1)S(1)} collective-permute-done((bf16[1,40,2048]{2,1,0:T(8,128)(2,1)}, bf16[1,40,2048]{2,1,0:T(8,128)(2,1)S(1)}, u32[]{:S(2)}, u32[]{:S(2)}) %collective-permute-start.7) | collective-permute-done | bytes 163872 | tf_op jit(solution)/shard_map/ppermute | solution.py:28
  158.0 8.3 %collective-permute-done.8 = bf16[1,40,2048]{2,1,0:T(8,128)(2,1)S(1)} collective-permute-done((bf16[1,40,2048]{2,1,0:T(8,128)(2,1)}, bf16[1,40,2048]{2,1,0:T(8,128)(2,1)S(1)}, u32[]{:S(2)}, u32[]{:S(2)}) %collective-permute-start.8) | collective-permute-done | bytes 163872 | tf_op jit(solution)/shard_map/ppermute | solution.py:28
  168.3 5.9 %collective-permute-done.9 = bf16[1,40,2048]{2,1,0:T(8,128)(2,1)S(1)} collective-permute-done((bf16[1,40,2048]{2,1,0:T(8,128)(2,1)S(1)}, bf16[1,40,2048]{2,1,0:T(8,128)(2,1)S(1)}, u32[]{:S(2)}, u32[]{:S(2)}) %collective-permute-start.9) | collective-permute-done | bytes 163872 | tf_op jit(solution)/shard_map/ppermute | solution.py:28
  174.2 4.7 %collective-permute-start.10 = (bf16[1,40,2048]{2,1,0:T(8,128)(2,1)S(1)}, bf16[1,40,2048]{2,1,0:T(8,128)(2,1)S(1)}, u32[]{:S(2)}, u32[]{:S(2)}) collective-permute-start(bf16[1,40,2048]{2,1,0:T(8,128)(2,1)S(1)} %get-tuple-element.22), channel_id=1, source_target_pairs={{0,11},{1,12},{2,13},{3,14},{4,15},{5,0},{6,1},{7,2},{8,3},{9,4},{... | collective-permute-start | bytes 491528 | tf_op jit(solution)/shard_map/ppermute | solution.py:28
  187.7 13.8 %fusion.16 = f32[640,2816]{1,0:T(8,128)} fusion(bf16[640,2048]{1,0:T(8,128)(2,1)} %bitcast.114, bf16[2816,2048]{1,0:T(8,128)(2,1)} %bitcast.119), kind=kOutput, calls=%fused_computation.88 | convolution fusion | flops 7381975040 | bytes 21364736 | tf_op jit(solution)/shard_map/dot_general | solution.py:42
  201.6 11.8 %multiply_reduce_fusion = (bf16[640]{0:T(1024)(128)(2,1)S(1)}, bf16[640,1408]{1,0:T(8,128)(2,1)S(1)}, bf16[640,1408]{1,0:T(8,128)(2,1)S(1)}, bf16[640,1408]{1,0:T(8,128)(2,1)}) fusion(f32[640,2816]{1,0:T(8,128)} %fusion.16, f32[640]{0:T(1024)S(1)} %reshape.169, bf16[640,2048]{1,0:T(8,128)(2,1)} %bitcast.4, ...), kind=kOutput, calls=%fused_computation.12 | convolution fusion | flops 3708108288 | bytes 21008128 | tf_op jit(solution)/shard_map/dot_general | solution.py:50
  213.4 10.2 %fusion.3 = f32[1408,2048]{1,0:T(8,128)} fusion(bf16[640,1408]{1,0:T(8,128)(2,1)S(1)} %get-tuple-element.13, bf16[640,2048]{1,0:T(8,128)(2,1)} %bitcast.4, f32[640]{0:T(1024)S(1)} %reshape.169), kind=kOutput, calls=%fused_computation.20 | convolution fusion | flops 3694919680 | bytes 15960576 | tf_op jit(solution)/shard_map/dot_general | solution.py:56
  223.9 3.6 fusion.5
  227.4 6.0 %copy.27 = bf16[2816,640]{1,0:T(8,128)(2,1)} copy(bf16[2816,640]{0,1:T(8,128)(2,1)} %fusion.5) | data formatting | bytes 7208960 | tf_op jit(solution)/shard_map/dot_general | solution.py:66
  233.5 16.6 %fusion.17 = f32[2,1408,2048]{2,1,0:T(8,128)} fusion(bf16[2,1408,640]{2,1,0:T(8,128)(2,1)} %bitcast.111, bf16[640,2048,1]{1,0,2:T(8,128)(2,1)S(1)} %bitcast.115), kind=kOutput, calls=%fused_computation.89 | convolution fusion | flops 7381975040 | bytes 29294592 | tf_op jit(solution)/shard_map/dot_general | solution.py:66
  250.8 12.1 %all-to-all-start.3 = ((bf16[16,1,40]{2,1,0:T(2,128)(2,1)}), bf16[16,1,40]{2,1,0:T(2,128)(2,1)S(1)}, u32[]{:S(2)}, u32[]{:S(2)}) async-start(bf16[16,1,40]{2,1,0:T(2,128)(2,1)} %convert_element_type.73), calls=%async_computation.3 | async-start | bytes 16384 | tf_op jit(solution)/shard_map/all_to_all | solution.py:133
  262.9 13.0 %convolution_convert_fusion = bf16[640,2048]{1,0:T(8,128)(2,1)} fusion(bf16[2816,2048]{1,0:T(8,128)(2,1)} %bitcast.120, bf16[640,1408]{1,0:T(8,128)(2,1)S(1)} %copy-done.3, bf16[640,1408]{1,0:T(8,128)(2,1)} %get-tuple-element.17), kind=kOutput, calls=%fused_computation.18 | convolution fusion | flops 7390494720 | bytes 17760256 | tf_op jit(solution)/shard_map/dot_general | solution.py:65
  276.0 6.9 %all-to-all-start.2 = ((bf16[16,40,2048]{2,1,0:T(8,128)(2,1)}), bf16[16,40,2048]{2,1,0:T(8,128)(2,1)S(1)}, u32[]{:S(2)}, u32[]{:S(2)}) async-start(bf16[16,40,2048]{2,1,0:T(8,128)(2,1)} %bitcast.113), calls=%async_computation.2 | async-start | bytes 5242880 | tf_op jit(solution)/shard_map/all_to_all | solution.py:126
  283.0 3.5 gather_fusion.5
  287.3 43.6 %all-to-all-done.2 = bf16[16,40,2048]{2,1,0:T(8,128)(2,1)S(1)} async-done(((bf16[16,40,2048]{2,1,0:T(8,128)(2,1)}), bf16[16,40,2048]{2,1,0:T(8,128)(2,1)S(1)}, u32[]{:S(2)}, u32[]{:S(2)}) %all-to-all-start.2) | async-done | bytes 2621472 | tf_op jit(solution)/shard_map/all_to_all | solution.py:126
  336.9 3.9 %reduce_sum.34 = bf16[128,2048]{1,0:T(8,128)(2,1)} reduce(bf16[128,4,2048]{2,1,0:T(4,128)(2,1)S(1)} %reshape.166, bf16[]{:T(256)} %constant.130.clone.1), dimensions={1}, to_apply=%region_4.5 | reduce | flops 786432 | bytes 2621442 | tf_op jit(solution)/shard_map/reduce_sum | solution.py:144
  340.8 4.7 %convert_bitcast_fusion.1 = bf16[1,704,2048]{2,1,0:T(8,128)(2,1)} fusion(f32[704,2048]{1,0:T(8,128)} %reduce-scatter.5.cloned.1.call-done), kind=kLoop, calls=%fused_computation.19 | loop fusion | flops 1441792 | bytes 8650752 | tf_op jit(solution)/shard_map/broadcast_in_dim | solution.py:150
  345.5 7.7 %convert_bitcast_fusion = bf16[1,2,704,2048]{3,2,1,0:T(8,128)(2,1)} fusion(f32[2,704,2048]{2,1,0:T(8,128)} %reduce-scatter.3.cloned.1.call-done), kind=kLoop, calls=%fused_computation.9 | loop fusion | flops 2883584 | bytes 17301504 | tf_op jit(solution)/shard_map/broadcast_in_dim | solution.py:149
  (102 shorter events, 39.5 us)
Async XLA Ops:
  7.2 0.8 copy-start.7
  7.2 1.1 copy-start.8
  7.2 180.6 %all-gather.5.cloned.1.call-start = ((), (), s32[]{:S(2)}) async-start(), calls=%async_computation.7 | async-start | bytes 17301504 | tf_op jit(solution)/shard_map/all_gather | solution.py:111
  7.9 17.4 %copy-start.4 = (bf16[128,2048]{1,0:T(8,128)(2,1)S(1)}, bf16[128,2048]{1,0:T(8,128)(2,1)}, u32[]{:S(2)}) copy-start(bf16[128,2048]{1,0:T(8,128)(2,1)} %param.6) | copy-start | bytes 1572868
  17.8 24.6 %all-to-all-start = ((bf16[16,1,40]{2,1,0:T(2,128)(2,1)}), bf16[16,1,40]{2,1,0:T(2,128)(2,1)S(1)}, u32[]{:S(2)}, u32[]{:S(2)}) async-start(bf16[16,1,40]{2,1,0:T(2,128)(2,1)} %all_to_all.21), calls=%async_computation | async-start | bytes 16384 | tf_op jit(solution)/shard_map/all_to_all | solution.py:108
  25.0 176.6 %all-gather.3.cloned.1.call-start = ((), (), s32[]{:S(2)}) async-start(), calls=%async_computation.6 | async-start | bytes 8650752 | tf_op jit(solution)/shard_map/all_gather | solution.py:112
  30.1 8.3 %copy-start.5 = (bf16[128,2048]{1,0:T(8,128)(2,1)S(1)}, bf16[128,2048]{1,0:T(8,128)(2,1)}, u32[]{:S(2)}) copy-start(bf16[128,2048]{1,0:T(8,128)(2,1)} %param.7) | copy-start | bytes 1572868
  30.1 154.5 %collective-permute-start.14 = (bf16[1,40,2048]{2,1,0:T(8,128)(2,1)S(1)}, bf16[1,40,2048]{2,1,0:T(8,128)(2,1)}, u32[]{:S(2)}, u32[]{:S(2)}) collective-permute-start(bf16[1,40,2048]{2,1,0:T(8,128)(2,1)S(1)} %get-tuple-element.18), channel_id=1, source_target_pairs={{0,15},{1,0},{2,1},{3,2},{4,3},{5,4},{6,5},{7,6},{8,7},{9,8},{10,9... | collective-permute-start | bytes 491528 | tf_op jit(solution)/shard_map/ppermute | solution.py:28
  31.5 152.1 %collective-permute-start.13 = (bf16[1,40,2048]{2,1,0:T(8,128)(2,1)S(1)}, bf16[1,40,2048]{2,1,0:T(8,128)(2,1)}, u32[]{:S(2)}, u32[]{:S(2)}) collective-permute-start(bf16[1,40,2048]{2,1,0:T(8,128)(2,1)S(1)} %get-tuple-element.19), channel_id=1, source_target_pairs={{0,14},{1,15},{2,0},{3,1},{4,2},{5,3},{6,4},{7,5},{8,6},{9,7},{10,... | collective-permute-start | bytes 491528 | tf_op jit(solution)/shard_map/ppermute | solution.py:28
  33.0 149.7 %collective-permute-start.12 = (bf16[1,40,2048]{2,1,0:T(8,128)(2,1)S(1)}, bf16[1,40,2048]{2,1,0:T(8,128)(2,1)}, u32[]{:S(2)}, u32[]{:S(2)}) collective-permute-start(bf16[1,40,2048]{2,1,0:T(8,128)(2,1)S(1)} %get-tuple-element.20), channel_id=1, source_target_pairs={{0,13},{1,14},{2,15},{3,0},{4,1},{5,2},{6,3},{7,4},{8,5},{9,6},{10... | collective-permute-start | bytes 491528 | tf_op jit(solution)/shard_map/ppermute | solution.py:28
  33.0 148.8 %collective-permute-start.11 = (bf16[1,40,2048]{2,1,0:T(8,128)(2,1)S(1)}, bf16[1,40,2048]{2,1,0:T(8,128)(2,1)}, u32[]{:S(2)}, u32[]{:S(2)}) collective-permute-start(bf16[1,40,2048]{2,1,0:T(8,128)(2,1)S(1)} %get-tuple-element.21), channel_id=1, source_target_pairs={{0,12},{1,13},{2,14},{3,15},{4,0},{5,1},{6,2},{7,3},{8,4},{9,5},{1... | collective-permute-start | bytes 491528 | tf_op jit(solution)/shard_map/ppermute | solution.py:28
  36.3 12.7 %collective-permute-start = (bf16[1,40,2048]{2,1,0:T(8,128)(2,1)}, bf16[1,40,2048]{2,1,0:T(8,128)(2,1)}, u32[]{:S(2)}, u32[]{:S(2)}) collective-permute-start(bf16[1,40,2048]{2,1,0:T(8,128)(2,1)} %get-tuple-element.32), channel_id=1, source_target_pairs={{0,1},{1,2},{2,3},{3,4},{4,5},{5,6},{6,7},{7,8},{8,9},{9,10},{10,1... | collective-permute-start | bytes 491528 | tf_op jit(solution)/shard_map/ppermute | solution.py:28
  42.5 8.0 %copy-start = (bf16[16,1,40,2048]{3,2,0,1:T(8,128)(2,1)S(1)}, bf16[16,1,40,2048]{3,2,0,1:T(8,128)(2,1)}, u32[]{:S(2)}) copy-start(bf16[16,1,40,2048]{3,2,0,1:T(8,128)(2,1)} %get-tuple-element.33) | copy-start | bytes 7864324
  42.5 159.1 %all-to-all-start.1 = ((bf16[16,40,2048]{2,1,0:T(8,128)(2,1)}), bf16[16,40,2048]{2,1,0:T(8,128)(2,1)}, u32[]{:S(2)}, u32[]{:S(2)}) async-start(bf16[16,40,2048]{2,1,0:T(8,128)(2,1)} %bitcast.3), calls=%async_computation.1 | async-start | bytes 5242880 | tf_op jit(solution)/shard_map/all_to_all | solution.py:107
  48.7 292.1 %reduce-scatter.5.cloned.1.call-start = ((), (), s32[]{:S(2)}) async-start(), calls=%async_computation.9 | async-start | bytes 17301504 | tf_op jit(solution)/shard_map/reduce_scatter | solution.py:123
  48.9 117.4 %copy-start.6 = (bf16[1,40,2048]{2,1,0:T(8,128)(2,1)S(1)}, bf16[1,40,2048]{2,1,0:T(8,128)(2,1)}, u32[]{:S(2)}) copy-start(bf16[1,40,2048]{2,1,0:T(8,128)(2,1)} %get-tuple-element.23) | copy-start | bytes 491524
  48.9 57.8 %collective-permute-start.1 = (bf16[1,40,2048]{2,1,0:T(8,128)(2,1)}, bf16[1,40,2048]{2,1,0:T(8,128)(2,1)S(1)}, u32[]{:S(2)}, u32[]{:S(2)}) collective-permute-start(bf16[1,40,2048]{2,1,0:T(8,128)(2,1)} %get-tuple-element.31), channel_id=1, source_target_pairs={{0,2},{1,3},{2,4},{3,5},{4,6},{5,7},{6,8},{7,9},{8,10},{9,11},{10,... | collective-permute-start | bytes 491528 | tf_op jit(solution)/shard_map/ppermute | solution.py:28
  106.8 9.2 %collective-permute-start.2 = (bf16[1,40,2048]{2,1,0:T(8,128)(2,1)}, bf16[1,40,2048]{2,1,0:T(8,128)(2,1)S(1)}, u32[]{:S(2)}, u32[]{:S(2)}) collective-permute-start(bf16[1,40,2048]{2,1,0:T(8,128)(2,1)} %get-tuple-element.30), channel_id=1, source_target_pairs={{0,3},{1,4},{2,5},{3,6},{4,7},{5,8},{6,9},{7,10},{8,11},{9,12},{10... | collective-permute-start | bytes 491528 | tf_op jit(solution)/shard_map/ppermute | solution.py:28
  116.0 6.4 %collective-permute-start.3 = (bf16[1,40,2048]{2,1,0:T(8,128)(2,1)}, bf16[1,40,2048]{2,1,0:T(8,128)(2,1)S(1)}, u32[]{:S(2)}, u32[]{:S(2)}) collective-permute-start(bf16[1,40,2048]{2,1,0:T(8,128)(2,1)} %get-tuple-element.29), channel_id=1, source_target_pairs={{0,4},{1,5},{2,6},{3,7},{4,8},{5,9},{6,10},{7,11},{8,12},{9,13},{1... | collective-permute-start | bytes 491528 | tf_op jit(solution)/shard_map/ppermute | solution.py:28
  122.4 8.3 %collective-permute-start.4 = (bf16[1,40,2048]{2,1,0:T(8,128)(2,1)}, bf16[1,40,2048]{2,1,0:T(8,128)(2,1)S(1)}, u32[]{:S(2)}, u32[]{:S(2)}) collective-permute-start(bf16[1,40,2048]{2,1,0:T(8,128)(2,1)} %get-tuple-element.28), channel_id=1, source_target_pairs={{0,5},{1,6},{2,7},{3,8},{4,9},{5,10},{6,11},{7,12},{8,13},{9,14},{... | collective-permute-start | bytes 491528 | tf_op jit(solution)/shard_map/ppermute | solution.py:28
  130.7 9.6 %collective-permute-start.5 = (bf16[1,40,2048]{2,1,0:T(8,128)(2,1)}, bf16[1,40,2048]{2,1,0:T(8,128)(2,1)S(1)}, u32[]{:S(2)}, u32[]{:S(2)}) collective-permute-start(bf16[1,40,2048]{2,1,0:T(8,128)(2,1)} %get-tuple-element.27), channel_id=1, source_target_pairs={{0,6},{1,7},{2,8},{3,9},{4,10},{5,11},{6,12},{7,13},{8,14},{9,15},... | collective-permute-start | bytes 491528 | tf_op jit(solution)/shard_map/ppermute | solution.py:28
  140.3 8.8 %collective-permute-start.6 = (bf16[1,40,2048]{2,1,0:T(8,128)(2,1)}, bf16[1,40,2048]{2,1,0:T(8,128)(2,1)S(1)}, u32[]{:S(2)}, u32[]{:S(2)}) collective-permute-start(bf16[1,40,2048]{2,1,0:T(8,128)(2,1)} %get-tuple-element.26), channel_id=1, source_target_pairs={{0,7},{1,8},{2,9},{3,10},{4,11},{5,12},{6,13},{7,14},{8,15},{9,0},... | collective-permute-start | bytes 491528 | tf_op jit(solution)/shard_map/ppermute | solution.py:28
  149.1 8.9 %collective-permute-start.7 = (bf16[1,40,2048]{2,1,0:T(8,128)(2,1)}, bf16[1,40,2048]{2,1,0:T(8,128)(2,1)S(1)}, u32[]{:S(2)}, u32[]{:S(2)}) collective-permute-start(bf16[1,40,2048]{2,1,0:T(8,128)(2,1)} %get-tuple-element.25), channel_id=1, source_target_pairs={{0,8},{1,9},{2,10},{3,11},{4,12},{5,13},{6,14},{7,15},{8,0},{9,1},... | collective-permute-start | bytes 491528 | tf_op jit(solution)/shard_map/ppermute | solution.py:28
  158.0 8.3 %collective-permute-start.8 = (bf16[1,40,2048]{2,1,0:T(8,128)(2,1)}, bf16[1,40,2048]{2,1,0:T(8,128)(2,1)S(1)}, u32[]{:S(2)}, u32[]{:S(2)}) collective-permute-start(bf16[1,40,2048]{2,1,0:T(8,128)(2,1)} %get-tuple-element.24), channel_id=1, source_target_pairs={{0,9},{1,10},{2,11},{3,12},{4,13},{5,14},{6,15},{7,0},{8,1},{9,2},... | collective-permute-start | bytes 491528 | tf_op jit(solution)/shard_map/ppermute | solution.py:28
  166.3 7.9 %collective-permute-start.9 = (bf16[1,40,2048]{2,1,0:T(8,128)(2,1)S(1)}, bf16[1,40,2048]{2,1,0:T(8,128)(2,1)S(1)}, u32[]{:S(2)}, u32[]{:S(2)}) collective-permute-start(bf16[1,40,2048]{2,1,0:T(8,128)(2,1)S(1)} %copy-done.6), channel_id=1, source_target_pairs={{0,10},{1,11},{2,12},{3,13},{4,14},{5,15},{6,0},{7,1},{8,2},{9,3},... | collective-permute-start | bytes 491528 | tf_op jit(solution)/shard_map/ppermute | solution.py:28
  174.2 7.6 %collective-permute-start.10 = (bf16[1,40,2048]{2,1,0:T(8,128)(2,1)S(1)}, bf16[1,40,2048]{2,1,0:T(8,128)(2,1)S(1)}, u32[]{:S(2)}, u32[]{:S(2)}) collective-permute-start(bf16[1,40,2048]{2,1,0:T(8,128)(2,1)S(1)} %get-tuple-element.22), channel_id=1, source_target_pairs={{0,11},{1,12},{2,13},{3,14},{4,15},{5,0},{6,1},{7,2},{8,3},{9,4},{... | collective-permute-start | bytes 491528 | tf_op jit(solution)/shard_map/ppermute | solution.py:28
  213.4 10.5 %copy-start.2 = (bf16[640,1408]{1,0:T(8,128)(2,1)}, bf16[640,1408]{1,0:T(8,128)(2,1)S(1)}, u32[]{:S(2)}) copy-start(bf16[640,1408]{1,0:T(8,128)(2,1)S(1)} %get-tuple-element.16) | copy-start | bytes 5406724
  223.6 121.9 %reduce-scatter.3.cloned.1.call-start = ((), (), s32[]{:S(2)}) async-start(), calls=%async_computation.8 | async-start | bytes 34603008 | tf_op jit(solution)/shard_map/reduce_scatter | solution.py:122
  227.4 6.0 %copy-start.1 = (bf16[16,40,2048]{2,1,0:T(8,128)(2,1)S(1)}, bf16[16,40,2048]{2,1,0:T(8,128)(2,1)}, u32[]{:S(2)}) copy-start(bf16[16,40,2048]{2,1,0:T(8,128)(2,1)} %gather_fusion.3) | copy-start | bytes 7864324
  250.1 12.8 %copy-start.3 = (bf16[640,1408]{1,0:T(8,128)(2,1)S(1)}, bf16[640,1408]{1,0:T(8,128)(2,1)}, u32[]{:S(2)}) copy-start(bf16[640,1408]{1,0:T(8,128)(2,1)} %copy-done.2) | copy-start | bytes 5406724
  250.8 25.1 %all-to-all-start.3 = ((bf16[16,1,40]{2,1,0:T(2,128)(2,1)}), bf16[16,1,40]{2,1,0:T(2,128)(2,1)S(1)}, u32[]{:S(2)}, u32[]{:S(2)}) async-start(bf16[16,1,40]{2,1,0:T(2,128)(2,1)} %convert_element_type.73), calls=%async_computation.3 | async-start | bytes 16384 | tf_op jit(solution)/shard_map/all_to_all | solution.py:133
  276.0 55.0 %all-to-all-start.2 = ((bf16[16,40,2048]{2,1,0:T(8,128)(2,1)}), bf16[16,40,2048]{2,1,0:T(8,128)(2,1)S(1)}, u32[]{:S(2)}, u32[]{:S(2)}) async-start(bf16[16,40,2048]{2,1,0:T(8,128)(2,1)} %bitcast.113), calls=%async_computation.2 | async-start | bytes 5242880 | tf_op jit(solution)/shard_map/all_to_all | solution.py:126
Sparse Core Ops, SparseCore 0:
  9.6 24.4 all-gather.4
  38.4 16.1 all-gather.2
  223.7 27.3 reduce-scatter.4
  253.2 36.3 reduce-scatter.2
